TPU v7x, 256 devices: a whole 4x4x8 slice. The times are simulated.
256 devices in a mesh: gossip: 16 (over z, x_lo), fsdp: 16 (over x_hi, y, core).
Axes of the slice: x: 4 (x_hi: 2, x_lo: 2; x = x_hi * 2 + x_lo), y: 4, z: 8, core: 2. Of those that a mesh axis runs over, the one named last changes fastest.
Arguments:
- inputs: bfloat16 [16, 2048, 2048], P('gossip', 'fsdp'), may hold values from -6 to 6
- out_grad: bfloat16 [16, 2048, 2048], P('gossip', 'fsdp'), may hold values from -6 to 6
- norm_gain: float32 [16, 2048], P('gossip'), may hold values from 0.5 to 1.5
- w_qkv: bfloat16 [16, 16, 2048, 384], P('gossip', 'fsdp'), may hold values from -64 to 64
- w_out: bfloat16 [16, 16, 128, 2048], P('gossip', 'fsdp'), may hold values from -6 to 6
- mom_qkv: bfloat16 [16, 16, 2048, 384], P('gossip', 'fsdp'), may hold values from -6 to 6
- mom_out: bfloat16 [16, 16, 128, 2048], P('gossip', 'fsdp'), may hold values from -6 to 6
- step_index: int32 [1], replicated, may hold values from 0 to 11
Outputs:
- new_qkv: bfloat16 [16, 16, 2048, 384], P('gossip', 'fsdp')
- new_out: bfloat16 [16, 16, 128, 2048], P('gossip', 'fsdp')
- new_mom_qkv: bfloat16 [16, 16, 2048, 384], P('gossip', 'fsdp')
- new_mom_out: bfloat16 [16, 16, 128, 2048], P('gossip', 'fsdp')
All inputs are finite; a program needn't handle non-finite values.
Results may differ from a plain program's by a relative error of at most 0.0085.
Values may be sent and summed in bfloat16 or wider, within the bound.
A program may use at most 128 MiB of HBM per device.

v0:
```python
from functools import partial
import math

import jax
import jax.numpy as jnp
from jax import lax
from jax.experimental import pallas as pl
from jax.experimental.pallas import tpu as pltpu
from jax.sharding import PartitionSpec as P

LEVELS = 3
BETA = 0.9
RATE = 0.1
EPSILON = 1e-05
MESH = pl.DeviceIdType.MESH
F32 = jnp.float32
BF16 = jnp.bfloat16

(UP, DOWN, ACROSS, SIB, U2, D2, S_LO, S_HI, C_UP, C_DOWN, C_SIB, AX1, AX2, S_F1, S_F2,
 S_OLO, S_OHI, S_OF1, S_OF2) = range(19)
PER_ARRAY = 19
WQ = 2 * PER_ARRAY
WO = WQ + 1
MO = WQ + 2
WO2 = WQ + 3
MO2 = WQ + 4
MQ = WQ + 5


def dot_nt(a, b):
    return lax.dot_general(a, b, (((1,), (1,)), ((), ())), preferred_element_type=F32)


def dot_tn(a, b):
    return lax.dot_general(a, b, (((0,), (0,)), ((), ())), preferred_element_type=F32)


def pick(i, values):
    out = jnp.int32(values[0])
    for k in range(1, len(values)):
        out = jnp.where(i == k, jnp.int32(values[k]), out)
    return out


def average(own, other):
    return ((own.astype(F32) + other.astype(F32)) * 0.5).astype(BF16)


def move(weight, moved_m, rate):
    return (weight.astype(F32) - rate * moved_m.astype(F32)).astype(BF16)


def kernel(by, rate_ref, gain_ref, hc_ref, hs_ref, lc_ref, ls_ref,
           x_ref, og_ref, wq_ref, wo_ref, mq_ref, mo_ref,
           nwq_ref, nwo_ref, nmq_ref, nmo_ref,
           ax, aog, n_s, wrel, mrel, wq_v, wo_v, mq_v, mo_v, pq_v, po_v, rq_v, ro_v,
           q_s, k_s, v_s, qt_s, kt_s, vt_s, att_t, o_s, s_s, p_s, go_s, dk_s, dv_s, gp_s,
           send_sem, recv_sem, loc_sem):
    g = lax.axis_index("gossip")
    f = lax.axis_index("fsdp")
    n_g = lax.axis_size("gossip")
    core = lax.rem(f, 2)
    y = lax.rem(f // 2, 4)
    xh = f // 8
    chunks, block, width = ax.shape
    rows = block // 2
    half = rows // 2
    head_dim = wo_v.shape[0]
    out_scale = 1.0 / math.sqrt(lax.axis_size("fsdp") * head_dim)
    in_scale = 1.0 / math.sqrt(width)
    scale = 1.0 / math.sqrt(head_dim)

    def dev(xx, yy, cc):
        return xx * 8 + lax.rem(yy + 4, 4) * 2 + cc

    up = (g, dev(xh, y + 1, core))
    down = (g, dev(xh, y - 1, core))
    sib = (g, dev(xh, y, 1 - core))
    across = (g, dev(1 - xh, y, core))
    partner = (lax.rem(g + by, n_g), f)
    source = (lax.rem(g - by + n_g, n_g), f)
    leg = 6
    relayed = n_g - by == 2 * leg
    ahead = (lax.rem(g - leg + n_g, n_g), f)
    behind = (lax.rem(g + leg, n_g), f)
    along_y = by == 1

    def chunk(side, yy):
        return side * 4 + lax.rem(yy + 4, 4)

    def piece(dst, side, yy, part=None):
        first = pl.multiple_of(core * rows, rows)
        if part is None:
            return dst.at[chunk(side, yy), pl.ds(first, rows)]
        return dst.at[chunk(side, yy), pl.ds(pl.multiple_of(first + part * half, half), half)]

    def remote(i, src, dst, target):
        return pltpu.make_async_remote_copy(
            src_ref=src, dst_ref=dst, send_sem=send_sem.at[i], recv_sem=recv_sem.at[i],
            device_id=target, device_id_type=MESH)

    arrays = ((x_ref, ax), (og_ref, aog))

    def copy(a, i):
        src, dst = arrays[a]
        own, other = xh, 1 - xh
        n = a * PER_ARRAY + i

        def same(where, target):
            return remote(n, where, where, target)

        if i in (UP, DOWN, ACROSS, SIB):
            return remote(n, src.at[0], piece(dst, own, y),
                          {UP: up, DOWN: down, ACROSS: across, SIB: sib}[i])
        if i == U2:
            return same(piece(dst, own, y - 1, 0), up)
        if i == D2:
            return same(piece(dst, own, y + 1, 1), down)
        if i == S_LO:
            return same(piece(dst, own, y - 1), sib)
        if i == S_HI:
            return same(piece(dst, own, y + 1), sib)
        if i in (C_UP, C_DOWN, C_SIB):
            return same(piece(dst, other, y), {C_UP: up, C_DOWN: down, C_SIB: sib}[i])
        if i == AX1:
            if along_y:
                return same(piece(dst, other, y - 1, 0), up)
            return same(piece(dst, own, y + 2, 0), across)
        if i == AX2:
            if along_y:
                return same(piece(dst, other, y + 1, 1), down)
            return same(piece(dst, own, y + 2, 1), across)
        if i == S_F1:
            return same(piece(dst, own, y + 2, 0), sib)
        if i == S_F2:
            return same(piece(dst, own, y + 2, 1), sib)
        if i == S_OLO:
            return same(piece(dst, other, y - 1), sib)
        if i == S_OHI:
            return same(piece(dst, other, y + 1), sib)
        if i == S_OF1:
            return same(piece(dst, other, y + 2, 0), sib)
        return same(piece(dst, other, y + 2, 1), sib)

    def start(a, *which):
        for i in which:
            copy(a, i).start()

    def arrived(a, *which):
        for i in which:
            copy(a, i).wait_recv()

    def local(i, src, dst):
        return pltpu.make_async_copy(src, dst, loc_sem.at[i])

    def own_copy(a):
        return local(a, arrays[a][0].at[0], piece(arrays[a][1], xh, y))

    loads = [local(2, wq_ref, wq_v), local(3, wo_ref, wo_v),
             local(4, mq_ref, mq_v), local(5, mo_ref, mo_v)]
    send_wq = remote(WQ, wq_ref, pq_v, partner)
    if relayed:
        send_wo = remote(WO, wo_ref, wrel, ahead)
        send_mo = remote(MO, mo_v, mrel, ahead)
        pass_wo = remote(WO2, wrel, po_v, ahead)
        pass_mo = remote(MO2, mrel, ro_v, ahead)
    else:
        send_wo = remote(WO, wo_ref, po_v, partner)
        send_mo = remote(MO, mo_v, ro_v, partner)

    def send_mq(d):
        at = pl.ds(pl.multiple_of(d * block, block), block)
        return remote(MQ + d, mq_v.at[at], rq_v.at[at], partner)

    own_copy(0).start()
    loads[0].start()
    barrier = pltpu.get_barrier_semaphore()
    everyone = [up, down, sib, across, partner, source]
    if relayed:
        everyone += [ahead, behind]
    for target in everyone:
        pl.semaphore_signal(barrier, inc=1, device_id=target, device_id_type=MESH)
    pl.semaphore_wait(barrier, len(everyone))
    start(0, UP, DOWN, ACROSS, SIB)
    if not along_y:
        send_wq.start()
        send_wo.start()
    own_copy(1).start()
    for c in loads[1:]:
        c.start()
    loads[0].wait()

    def near(a):
        arrived(a, UP)
        start(a, U2, S_LO)
        arrived(a, DOWN)
        start(a, D2, S_HI)

    def row(a):
        arrived(a, ACROSS)
        start(a, C_UP, C_DOWN, C_SIB)

    def far(a):
        arrived(a, U2)
        start(a, *((S_F1,) if along_y else (AX1, S_F1)))
        arrived(a, D2)
        start(a, *((S_F2,) if along_y else (AX2, S_F2)))

    def other_near(a):
        arrived(a, C_UP)
        start(a, *((AX1, S_OLO) if along_y else (S_OLO,)))
        arrived(a, C_DOWN)
        start(a, *((AX2, S_OHI) if along_y else (S_OHI,)))

    def other_far(a):
        arrived(a, AX1)
        start(a, S_OF1)
        arrived(a, AX2)
        start(a, S_OF2)

    def second_array(late):
        if along_y and not late:
            start(1, ACROSS)
            send_wq.start()
            send_wo.start()
        if late == along_y:
            start(1, *((UP, DOWN, SIB) if along_y else (UP, DOWN, ACROSS, SIB)))

    def when(i, k, *steps):
        @pl.when(i == k)
        def _():
            for s in steps:
                s()

    def chunk_at(i):
        side = pick(i, (0, 0, 0, 1, 0, 1, 1, 1))
        move_y = pick(i, (0, 3, 1, 0, 2, 3, 1, 2))
        return lax.rem(xh + side, 2) * 4 + lax.rem(y + move_y, 4)

    def tables(m):
        hc, hs = hc_ref[pl.ds(m, 1), :], hs_ref[pl.ds(m, 1), :]
        lc, ls = lc_ref[...], ls_ref[...]
        return hc * lc - hs * ls, hs * lc + hc * ls

    def turned(t):
        return pltpu.roll(t, head_dim // 2, 1)

    def project(i, _):
        when(i, 0, lambda: own_copy(0).wait(), lambda: arrived(0, SIB))
        when(i, 1, lambda: near(0), lambda: row(0), lambda: arrived(0, S_LO))
        when(i, 2, lambda: arrived(0, S_HI))
        when(i, 3, lambda: far(0), lambda: second_array(False), lambda: arrived(0, C_SIB))
        when(i, 4, lambda: arrived(0, S_F1, S_F2))
        when(i, 5, lambda: other_near(0), lambda: second_array(True), lambda: arrived(0, S_OLO))
        when(i, 6, lambda: other_far(0), lambda: arrived(0, S_OHI))
        when(i, 7, lambda: arrived(0, S_OF1, S_OF2))
        m = chunk_at(i)

        columns = [slice(c, c + head_dim) for c in range(0, width, head_dim)]
        squares = jnp.zeros((block, head_dim), F32)
        for at in columns:
            t = ax[m, :, at].astype(F32)
            squares = squares + t * t
        stats = lax.rsqrt(jnp.sum(squares, -1, keepdims=True) * (1.0 / width) + EPSILON)
        for at in columns:
            n_s[m, :, at] = (ax[m, :, at].astype(F32) * stats * gain_ref[:, at]).astype(BF16)
        proj = jnp.dot(n_s[m], wq_v[...], preferred_element_type=F32) * in_scale
        cos, sin = tables(m)
        q = proj[:, :head_dim]
        k = proj[:, head_dim:2 * head_dim]
        q = (q * cos + turned(q) * sin).astype(BF16)
        k = (k * cos + turned(k) * sin).astype(BF16)
        v = proj[:, 2 * head_dim:].astype(BF16)
        q_s[m], k_s[m], v_s[m] = q, k, v
        qt_s[m], kt_s[m], vt_s[m] = q.T, k.T, v.T
        dk_s[m] = jnp.zeros_like(dk_s[m])
        dv_s[m] = jnp.zeros_like(dv_s[m])
        return 0

    lax.fori_loop(0, chunks, project, 0)

    row_pos = lax.broadcasted_iota(jnp.int32, (block, block), 0)
    col_pos = lax.broadcasted_iota(jnp.int32, (block, block), 1)

    def folded(t, op):
        return op(t.reshape(block // 8, 8, block), axis=0)

    def forward(m, _):
        if relayed:
            when(m, 1, send_wo.wait_recv, pass_wo.start)
        when(m, 5, lambda: near(1), lambda: row(1))
        queries = qt_s[m]

        def scores(j, top):
            for u in (2 * j, 2 * j + 1):
                s = jnp.dot(k_s[u], queries, preferred_element_type=F32) * scale
                s = jnp.where(row_pos + u * block <= col_pos + m * block, s, -jnp.inf)
                s_s[u] = s
                top = jnp.maximum(top, folded(s, jnp.max))
            return top

        top = lax.fori_loop(0, (m + 2) // 2, scores, jnp.full((8, block), -jnp.inf, F32))
        top = jnp.max(top, 0, keepdims=True)

        def exps(j, total):
            for u in (2 * j, 2 * j + 1):
                e = jnp.exp(s_s[u] - top)
                s_s[u] = e
                total = total + folded(e, jnp.sum)
            return total

        total = lax.fori_loop(0, (m + 2) // 2, exps, jnp.zeros((8, block), F32))
        inverse = 1.0 / jnp.sum(total, 0, keepdims=True)

        def values(j, out):
            for u in (2 * j, 2 * j + 1):
                p = (s_s[u] * inverse).astype(BF16)
                p_s[m, u] = p
                out = out + jnp.dot(vt_s[u], p, preferred_element_type=F32)
            return out

        out = lax.fori_loop(0, (m + 2) // 2, values, jnp.zeros((head_dim, block), F32))
        o_s[m] = out
        att_t[m] = out.astype(BF16)
        return 0

    lax.fori_loop(0, chunks, forward, 0)
    for c in loads[1:]:
        c.wait()
    go_s[...] = jnp.zeros_like(go_s)

    def backward(i, _):
        when(i, 0, lambda: own_copy(1).wait(), lambda: arrived(1, SIB))
        when(i, 1, lambda: far(1), lambda: arrived(1, S_LO))
        when(i, 2, lambda: arrived(1, S_HI))
        when(i, 3, lambda: arrived(1, C_SIB))
        when(i, 4, lambda: arrived(1, S_F1, S_F2), lambda: other_near(1))
        when(i, 5, lambda: arrived(1, S_OLO))
        when(i, 6, lambda: arrived(1, S_OHI))
        when(i, 7, lambda: other_far(1), lambda: arrived(1, S_OF1, S_OF2))
        m = chunk_at(i)
        da = (dot_nt(aog[m], wo_v[...]) * out_scale).astype(BF16)
        da_t = da.T
        go_s[...] += jnp.dot(att_t[m], aog[m], preferred_element_type=F32)

        @pl.when(i == chunks - 1)
        def _():
            def moved(r, _):
                at = pl.ds(pl.multiple_of(r * 16, 16), 16)
                grad = (go_s[at, :] * out_scale).astype(BF16)
                mo_v[at, :] = (BETA * mo_v[at, :].astype(F32) + grad.astype(F32)).astype(BF16)
                return 0

            lax.fori_loop(0, head_dim // 16, moved, 0)
            send_mo.start()

        centre = jnp.sum(da_t.astype(F32) * o_s[m], 0, keepdims=True)
        q = q_s[m]

        def pair(j, dq):
            for u in (2 * j, 2 * j + 1):
                p = p_s[m, u]
                dp = jnp.dot(v_s[u], da_t, preferred_element_type=F32)
                ds = (p.astype(F32) * (dp - centre) * scale).astype(BF16)
                dk_s[u] += jnp.dot(ds, q, preferred_element_type=F32)
                dv_s[u] += jnp.dot(p, da, preferred_element_type=F32)
                dq = dq + jnp.dot(kt_s[u], ds, preferred_element_type=F32)
            return dq

        dq = lax.fori_loop(0, (m + 2) // 2, pair, jnp.zeros((head_dim, block), F32)).T
        cos, sin = tables(m)
        gp_s[m, :, :head_dim] = ((dq * cos - turned(dq) * sin) * in_scale).astype(BF16)
        return 0

    lax.fori_loop(0, chunks, backward, 0)

    def finish(m, _):
        cos, sin = tables(m)
        dk = dk_s[m]
        gp_s[m, :, head_dim:2 * head_dim] = (
            (dk * cos - turned(dk) * sin) * in_scale).astype(BF16)
        gp_s[m, :, 2 * head_dim:] = (dv_s[m] * in_scale).astype(BF16)
        return 0

    lax.fori_loop(0, chunks, finish, 0)

    def grads(d, _):
        at = pl.ds(pl.multiple_of(d * block, block), block)
        total = dot_tn(n_s[0, :, at], gp_s[0])
        for m in range(1, chunks):
            total = total + dot_tn(n_s[m, :, at], gp_s[m])
        mq_v[at, :] = (BETA * mq_v[at, :].astype(F32)
                       + total.astype(BF16).astype(F32)).astype(BF16)
        send_mq(d).start()
        return 0

    lax.fori_loop(0, width // block, grads, 0)
    rate = rate_ref[0]
    send_wq.wait()
    if relayed:
        send_wo.wait_send()
        pass_wo.wait()
        send_mo.wait()
        pass_mo.start()
    else:
        send_wo.wait()
        send_mo.wait()

    def outs_o(r, _):
        at = pl.ds(pl.multiple_of(r * 16, 16), 16)
        mine, theirs = mo_v[at, :], ro_v[at, :]
        nmo_ref[at, :] = average(mine, theirs)
        nwo_ref[at, :] = average(move(wo_v[at, :], mine, rate), move(po_v[at, :], theirs, rate))
        return 0

    if not relayed:
        lax.fori_loop(0, head_dim // 16, outs_o, 0)

    def outs_q(d, _):
        send_mq(d).wait()
        at = pl.ds(pl.multiple_of(d * block, block), block)
        mine, theirs = mq_v[at, :], rq_v[at, :]
        nmq_ref[at, :] = average(mine, theirs)
        nwq_ref[at, :] = average(move(wq_v[at, :], mine, rate), move(pq_v[at, :], theirs, rate))
        return 0

    lax.fori_loop(0, width // block, outs_q, 0)
    if relayed:
        pass_mo.wait()
        lax.fori_loop(0, head_dim // 16, outs_o, 0)

    for a in range(2):
        for i in range(PER_ARRAY):
            copy(a, i).wait_send()


def update(by, cid, rate, gain, tables, x, og, wq, wo, mq, mo):
    devices = lax.axis_size("fsdp")
    rows, width = x.shape[1:]
    block = 2 * rows
    chunks = devices // 2
    wide, head_dim = wq.shape[1], wo.shape[0]
    hbm = pl.BlockSpec(memory_space=pl.ANY)
    vmem = pl.BlockSpec(memory_space=pltpu.VMEM)
    n_copies = MQ + width // block

    def v(*shape, dtype=BF16):
        return pltpu.VMEM(shape, dtype)

    return pl.pallas_call(
        partial(kernel, by),
        out_shape=(
            jax.ShapeDtypeStruct(wq.shape, BF16), jax.ShapeDtypeStruct(wo.shape, BF16),
            jax.ShapeDtypeStruct(wq.shape, BF16), jax.ShapeDtypeStruct(wo.shape, BF16),
        ),
        in_specs=[pl.BlockSpec(memory_space=pltpu.SMEM)] + [vmem] * 5 + [hbm] * 6,
        out_specs=[vmem] * 4,
        scratch_shapes=[
            v(chunks, block, width), v(chunks, block, width), v(chunks, block, width),
            v(head_dim, width), v(head_dim, width),
            v(width, wide), v(head_dim, width), v(width, wide), v(head_dim, width),
            v(width, wide), v(head_dim, width), v(width, wide), v(head_dim, width),
            v(chunks, block, head_dim), v(chunks, block, head_dim), v(chunks, block, head_dim),
            v(chunks, head_dim, block), v(chunks, head_dim, block), v(chunks, head_dim, block),
            v(chunks, head_dim, block), v(chunks, head_dim, block, dtype=F32),
            v(chunks, block, block, dtype=F32), v(chunks, chunks, block, block),
            v(head_dim, width, dtype=F32),
            v(chunks, block, head_dim, dtype=F32), v(chunks, block, head_dim, dtype=F32),
            v(chunks, block, wide),
            pltpu.SemaphoreType.DMA((n_copies,)), pltpu.SemaphoreType.DMA((n_copies,)),
            pltpu.SemaphoreType.DMA((6,)),
        ],
        name=f"update_{by}",
        compiler_params=pltpu.CompilerParams(
            collective_id=cid, has_side_effects=True, vmem_limit_bytes=66_000_000),
    )(rate, gain, *tables, x, og, wq, wo, mq, mo)


def per_device(inputs, out_grad, norm_gain, w_qkv, w_out, mom_qkv, mom_out, step_index):
    rate = RATE * (step_index.astype(F32) + 1.0) / (4.0 * LEVELS)
    exponent = jnp.remainder(step_index[0], LEVELS)
    head_dim = w_out.shape[2]
    rows = inputs.shape[1]
    block, chunks = 2 * rows, lax.axis_size("fsdp") // 2
    half_width = head_dim // 2
    frequency = jnp.exp(
        -math.log(10000.0) * 2.0 * jnp.arange(half_width, dtype=F32) / head_dim)
    frequency = jnp.concatenate([frequency, frequency])
    high = (jnp.arange(chunks) * block).astype(F32)[:, None] * frequency[None, :]
    low = jnp.arange(block).astype(F32)[:, None] * frequency[None, :]
    sign = jnp.where(jnp.arange(head_dim) < half_width, -1.0, 1.0).astype(F32)
    tables = (jnp.cos(high), jnp.sin(high) * sign, jnp.cos(low), jnp.sin(low) * sign)
    outs = lax.switch(
        exponent, [partial(update, 1 << k, k) for k in range(LEVELS)],
        rate, norm_gain, tables, inputs, out_grad,
        w_qkv[0, 0], w_out[0, 0], mom_qkv[0, 0], mom_out[0, 0])
    return tuple(o[None, None] for o in outs)


def solution(mesh):
    return jax.shard_map(
        per_device,
        mesh=mesh,
        in_specs=(
            P("gossip", "fsdp", None),
            P("gossip", "fsdp", None),
            P("gossip", None),
            P("gossip", "fsdp", None, None),
            P("gossip", "fsdp", None, None),
            P("gossip", "fsdp", None, None),
            P("gossip", "fsdp", None, None),
            P(),
        ),
        out_specs=(
            P("gossip", "fsdp", None, None),
            P("gossip", "fsdp", None, None),
            P("gossip", "fsdp", None, None),
            P("gossip", "fsdp", None, None),
        ),
        check_vma=False,
    )
```

profile of v0, /device:TPU:5, one launch (start us, length us, event | category | flops | bytes accessed | tf_op | source)
XLA Modules:
  0.0 173.6 jit_solution(9890752151219723144)
XLA Ops:
  1.3 0.1 pad_maximum_fusion
  1.4 0.1 broadcast_multiply_fusion.1
  1.5 0.1 broadcast_multiply_fusion
  1.6 166.2 %conditional.1 = ((bf16[2048,384]{1,0:T(8,128)(2,1)}, bf16[128,2048]{1,0:T(8,128)(2,1)S(1)}, bf16[2048,384]{1,0:T(8,128)(2,1)}, bf16[128,2048]{1,0:T(8,128)(2,1)})) conditional(s32[]{:T(128)} %clamp.3, (f32[1]{0:T(128)}, f32[8,128]{1,0:T(8,128)S(1)}, f32[128]{0:T(128)S(1)}, f32[256,128]{1,0:T(8,128)S(1)}, f32[128]{0:T(128)S(1)}, ...), branch_computations={%region_0.1_spmd, %region_1.2_spmd, %region_2.3_spmd} | conditional | flops 33794 | bytes 406560 | solution.py:493
  1.6 0.6 sine_multiply_fusion.1
  2.2 1.2 sine_multiply_fusion
  3.4 164.1 %update_1.2 = (bf16[2048,384]{1,0:T(8,128)(2,1)}, bf16[128,2048]{1,0:T(8,128)(2,1)S(1)}, bf16[2048,384]{1,0:T(8,128)(2,1)}, bf16[128,2048]{1,0:T(8,128)(2,1)}) custom-call(f32[1]{0:T(128)S(6)} %div.1.rate_ref, f32[1,2048]{1,0:T(1,128)} %get-tuple-element.230.gain_ref, f32[8,128]{1,0:T(8,128)} %get-tuple-element.289.hc_ref, ...), custom_call_target="tpu_custom_call" | custom-call | tf_op jit(solution)/shard_map/cond/branch_0_fun/update_1/pallas_call | solution.py:450
  167.8 0.0 copy-start
  167.8 2.8 %copy.29 = bf16[1,1,2048,384]{3,2,1,0:T(8,128)(2,1)} copy(bf16[1,1,2048,384]{3,2,1,0:T(8,128)(2,1)} %bitcast.29) | data formatting | bytes 3145728
  170.6 0.8 copy.30
  171.4 0.0 copy-done
  171.4 0.0 copy-start.1
  171.4 1.1 copy.31
  172.6 0.3 copy-done.1
  172.8 0.8 copy.32
  (4 shorter events, 0.0 us)
Async XLA Ops:
  167.8 3.6 %copy-start = (bf16[2048,384]{1,0:T(8,128)(2,1)S(1)}, bf16[2048,384]{1,0:T(8,128)(2,1)}, u32[]{:S(2)}) copy-start(bf16[2048,384]{1,0:T(8,128)(2,1)} %get-tuple-element.283) | copy-start | bytes 4718596
  171.4 1.4 copy-start.1
where the time goes:
time: 172 us; the launch traced here: 174 us
  Pallas kernels  164 us (95%)
  local copies, waits for them, and re-layouts  5.81 us (3%)
  other arithmetic  2.07 us (1%)
    pallas_call x1, Pallas kernels, update(): pl.pallas_call(partial(kernel, by), out_shape=(jax.ShapeDtypeStruct(wq.sh...  164 us
    unnamed x8, local copies, waits for them, and re-layouts  5.81 us

commit v1 on v0

--- a/solution.py
+++ b/solution.py
@@ -12,13 +12,14 @@
 BETA = 0.9
 RATE = 0.1
 EPSILON = 1e-05
+FINE = 16
 MESH = pl.DeviceIdType.MESH
 F32 = jnp.float32
 BF16 = jnp.bfloat16
 
-(UP, DOWN, ACROSS, SIB, U2, D2, S_LO, S_HI, C_UP, C_DOWN, C_SIB, AX1, AX2, S_F1, S_F2,
- S_OLO, S_OHI, S_OF1, S_OF2) = range(19)
-PER_ARRAY = 19
+(UP, UP_B, DOWN, DOWN_B, ACROSS, SIB, U2, D2, S_LO, S_HI, C_UP, C_DOWN, C_SIB, AX1, AX2, S_F1, S_F2,
+ S_OLO, S_OHI, S_OF1, S_OF2) = range(21)
+PER_ARRAY = 21
 WQ = 2 * PER_ARRAY
 WO = WQ + 1
 MO = WQ + 2
@@ -50,11 +51,11 @@
     return (weight.astype(F32) - rate * moved_m.astype(F32)).astype(BF16)
 
 
-def kernel(by, rate_ref, gain_ref, hc_ref, hs_ref, lc_ref, ls_ref,
+def kernel(by, rate_ref, gain_ref, tab_ref,
            x_ref, og_ref, wq_ref, wo_ref, mq_ref, mo_ref,
            nwq_ref, nwo_ref, nmq_ref, nmo_ref,
            ax, aog, n_s, wrel, mrel, wq_v, wo_v, mq_v, mo_v, pq_v, po_v, rq_v, ro_v,
-           q_s, k_s, v_s, qt_s, kt_s, vt_s, att_t, o_s, s_s, p_s, go_s, dk_s, dv_s, gp_s,
+           lc_s, ls_s, q_s, k_s, v_s, qt_s, kt_s, vt_s, att_t, o_s, s_s, p_s, go_s, dk_s, dv_s, gp_s,
            send_sem, recv_sem, loc_sem):
     g = lax.axis_index("gossip")
     f = lax.axis_index("fsdp")
@@ -109,9 +110,12 @@
         def same(where, target):
             return remote(n, where, where, target)
 
-        if i in (UP, DOWN, ACROSS, SIB):
-            return remote(n, src.at[0], piece(dst, own, y),
-                          {UP: up, DOWN: down, ACROSS: across, SIB: sib}[i])
+        if i in (ACROSS, SIB):
+            return remote(n, src.at[0], piece(dst, own, y), {ACROSS: across, SIB: sib}[i])
+        if i in (UP, UP_B, DOWN, DOWN_B):
+            part = 0 if i in (UP, DOWN_B) else 1
+            return remote(n, src.at[0, pl.ds(part * half, half)], piece(dst, own, y, part),
+                          up if i in (UP, UP_B) else down)
         if i == U2:
             return same(piece(dst, own, y - 1, 0), up)
         if i == D2:
@@ -181,7 +185,7 @@
     for target in everyone:
         pl.semaphore_signal(barrier, inc=1, device_id=target, device_id_type=MESH)
     pl.semaphore_wait(barrier, len(everyone))
-    start(0, UP, DOWN, ACROSS, SIB)
+    start(0, UP, DOWN, UP_B, DOWN_B, ACROSS, SIB)
     if not along_y:
         send_wq.start()
         send_wo.start()
@@ -189,12 +193,25 @@
     for c in loads[1:]:
         c.start()
     loads[0].wait()
+    step = block // FINE
+    fc, fs = tab_ref[0, pl.ds(chunks + FINE, step), :], tab_ref[1, pl.ds(chunks + FINE, step), :]
+    for c in range(FINE):
+        at = pl.ds(c * step, step)
+        cc, cs = tab_ref[0, pl.ds(chunks + c, 1), :], tab_ref[1, pl.ds(chunks + c, 1), :]
+        lc_s[at, :] = cc * fc - cs * fs
+        ls_s[at, :] = cs * fc + cc * fs
 
     def near(a):
         arrived(a, UP)
-        start(a, U2, S_LO)
+        start(a, U2)
         arrived(a, DOWN)
-        start(a, D2, S_HI)
+        start(a, D2)
+
+    def near_rest(a):
+        arrived(a, UP_B)
+        start(a, S_LO)
+        arrived(a, DOWN_B)
+        start(a, S_HI)
 
     def row(a):
         arrived(a, ACROSS)
@@ -224,7 +241,7 @@
             send_wq.start()
             send_wo.start()
         if late == along_y:
-            start(1, *((UP, DOWN, SIB) if along_y else (UP, DOWN, ACROSS, SIB)))
+            start(1, UP, DOWN, UP_B, DOWN_B, *((SIB,) if along_y else (ACROSS, SIB)))
 
     def when(i, k, *steps):
         @pl.when(i == k)
@@ -238,21 +255,23 @@
         return lax.rem(xh + side, 2) * 4 + lax.rem(y + move_y, 4)
 
     def tables(m):
-        hc, hs = hc_ref[pl.ds(m, 1), :], hs_ref[pl.ds(m, 1), :]
-        lc, ls = lc_ref[...], ls_ref[...]
+        hc, hs = tab_ref[0, pl.ds(m, 1), :], tab_ref[1, pl.ds(m, 1), :]
+        lc, ls = lc_s[...], ls_s[...]
         return hc * lc - hs * ls, hs * lc + hc * ls
 
     def turned(t):
         return pltpu.roll(t, head_dim // 2, 1)
 
     def project(i, _):
-        when(i, 0, lambda: own_copy(0).wait(), lambda: arrived(0, SIB))
-        when(i, 1, lambda: near(0), lambda: row(0), lambda: arrived(0, S_LO))
+        when(i, 0, lambda: own_copy(0).wait(), lambda: arrived(0, SIB),
+             lambda: near(0))
+        when(i, 1, lambda: near_rest(0), lambda: row(0), lambda: arrived(0, S_LO))
         when(i, 2, lambda: arrived(0, S_HI))
         when(i, 3, lambda: far(0), lambda: second_array(False), lambda: arrived(0, C_SIB))
         when(i, 4, lambda: arrived(0, S_F1, S_F2))
         when(i, 5, lambda: other_near(0), lambda: second_array(True), lambda: arrived(0, S_OLO))
-        when(i, 6, lambda: other_far(0), lambda: arrived(0, S_OHI))
+        when(i, 7 if along_y else 6, lambda: other_far(0))
+        when(i, 6, lambda: arrived(0, S_OHI))
         when(i, 7, lambda: arrived(0, S_OF1, S_OF2))
         m = chunk_at(i)
 
@@ -288,7 +307,10 @@
     def forward(m, _):
         if relayed:
             when(m, 1, send_wo.wait_recv, pass_wo.start)
-        when(m, 5, lambda: near(1), lambda: row(1))
+        when(m, 4 if along_y else 0, lambda: near(1))
+        when(m, 7 if along_y else 5, lambda: near_rest(1), lambda: row(1))
+        if not along_y:
+            when(m, 7, lambda: far(1))
         queries = qt_s[m]
 
         def scores(j, top):
@@ -331,13 +353,16 @@
 
     def backward(i, _):
         when(i, 0, lambda: own_copy(1).wait(), lambda: arrived(1, SIB))
-        when(i, 1, lambda: far(1), lambda: arrived(1, S_LO))
+        when(i, 1, lambda: arrived(1, S_LO))
         when(i, 2, lambda: arrived(1, S_HI))
+        if along_y:
+            when(i, 3, lambda: far(1))
         when(i, 3, lambda: arrived(1, C_SIB))
-        when(i, 4, lambda: arrived(1, S_F1, S_F2), lambda: other_near(1))
-        when(i, 5, lambda: arrived(1, S_OLO))
+        when(i, 4, lambda: arrived(1, S_F1, S_F2))
+        when(i, 5, lambda: other_near(1), lambda: arrived(1, S_OLO))
+        when(i, 7 if along_y else 6, lambda: other_far(1))
         when(i, 6, lambda: arrived(1, S_OHI))
-        when(i, 7, lambda: other_far(1), lambda: arrived(1, S_OF1, S_OF2))
+        when(i, 7, lambda: arrived(1, S_OF1, S_OF2))
         m = chunk_at(i)
         da = (dot_nt(aog[m], wo_v[...]) * out_scale).astype(BF16)
         da_t = da.T
@@ -453,13 +478,14 @@
             jax.ShapeDtypeStruct(wq.shape, BF16), jax.ShapeDtypeStruct(wo.shape, BF16),
             jax.ShapeDtypeStruct(wq.shape, BF16), jax.ShapeDtypeStruct(wo.shape, BF16),
         ),
-        in_specs=[pl.BlockSpec(memory_space=pltpu.SMEM)] + [vmem] * 5 + [hbm] * 6,
+        in_specs=[pl.BlockSpec(memory_space=pltpu.SMEM)] + [vmem] * 2 + [hbm] * 6,
         out_specs=[vmem] * 4,
         scratch_shapes=[
             v(chunks, block, width), v(chunks, block, width), v(chunks, block, width),
             v(head_dim, width), v(head_dim, width),
             v(width, wide), v(head_dim, width), v(width, wide), v(head_dim, width),
             v(width, wide), v(head_dim, width), v(width, wide), v(head_dim, width),
+            v(block, head_dim, dtype=F32), v(block, head_dim, dtype=F32),
             v(chunks, block, head_dim), v(chunks, block, head_dim), v(chunks, block, head_dim),
             v(chunks, head_dim, block), v(chunks, head_dim, block), v(chunks, head_dim, block),
             v(chunks, head_dim, block), v(chunks, head_dim, block, dtype=F32),
@@ -473,7 +499,7 @@
         name=f"update_{by}",
         compiler_params=pltpu.CompilerParams(
             collective_id=cid, has_side_effects=True, vmem_limit_bytes=66_000_000),
-    )(rate, gain, *tables, x, og, wq, wo, mq, mo)
+    )(rate, gain, tables, x, og, wq, wo, mq, mo)
 
 
 def per_device(inputs, out_grad, norm_gain, w_qkv, w_out, mom_qkv, mom_out, step_index):
@@ -486,10 +512,12 @@
     frequency = jnp.exp(
         -math.log(10000.0) * 2.0 * jnp.arange(half_width, dtype=F32) / head_dim)
     frequency = jnp.concatenate([frequency, frequency])
-    high = (jnp.arange(chunks) * block).astype(F32)[:, None] * frequency[None, :]
-    low = jnp.arange(block).astype(F32)[:, None] * frequency[None, :]
+    step = block // FINE
+    positions = jnp.concatenate(
+        [jnp.arange(chunks) * block, jnp.arange(FINE) * step, jnp.arange(step)])
+    angles = positions.astype(F32)[:, None] * frequency[None, :]
     sign = jnp.where(jnp.arange(head_dim) < half_width, -1.0, 1.0).astype(F32)
-    tables = (jnp.cos(high), jnp.sin(high) * sign, jnp.cos(low), jnp.sin(low) * sign)
+    tables = jnp.stack([jnp.cos(angles), jnp.sin(angles) * sign])
     outs = lax.switch(
         exponent, [partial(update, 1 << k, k) for k in range(LEVELS)],
         rate, norm_gain, tables, inputs, out_grad,

time: 172 us -> 168 us (0.977)
  other arithmetic: 2.07 us -> 0.33 us
    mul x4 -> x2, other arithmetic: 1.98 us -> 0.01 us  [the longest x1 0.01 us: per_device(): jnp.arange(FINE) * step]
where the time goes in v1:
time: 168 us; the launch traced here: 170 us
  Pallas kernels  163 us (97%)
  local copies, waits for them, and re-layouts  5.81 us (3%)
    pallas_call x1, Pallas kernels, update(): pl.pallas_call(partial(kernel, by), out_shape=(jax.ShapeDtypeStruct(wq.sh...  163 us
    unnamed x8, local copies, waits for them, and re-layouts  5.81 us

profile of v1, /device:TPU:5, one launch (start us, length us, event | category | flops | bytes accessed | tf_op | source)
XLA Modules:
  0.0 170.3 jit_solution(13216083984371430007)
XLA Ops:
  1.3 0.1 add_convert_fusion
  1.4 0.1 compare_select_fusion
  1.5 0.2 multiply_cosine_fusion
  1.7 162.8 %conditional.1 = ((bf16[2048,384]{1,0:T(8,128)(2,1)}, bf16[128,2048]{1,0:T(8,128)(2,1)S(1)}, bf16[2048,384]{1,0:T(8,128)(2,1)}, bf16[128,2048]{1,0:T(8,128)(2,1)})) conditional(s32[]{:T(128)} %clamp.3, (f32[1]{0:T(128)}, bf16[1,1,2048,384]{3,2,1,0:T(8,128)(2,1)}, bf16[1,1,128,2048]{3,2,1,0:T(8,128)(2,1)}, ...), branch_computations={%region_0.1_spmd, %region_1.2_spmd, %region_2.3_spmd} | conditional | flops 2 | bytes 32 | solution.py:521
  1.7 162.5 %update_1.2 = (bf16[2048,384]{1,0:T(8,128)(2,1)}, bf16[128,2048]{1,0:T(8,128)(2,1)S(1)}, bf16[2048,384]{1,0:T(8,128)(2,1)}, bf16[128,2048]{1,0:T(8,128)(2,1)}) custom-call(f32[1]{0:T(128)S(6)} %div.1.rate_ref, f32[1,2048]{1,0:T(1,128)} %get-tuple-element.149.gain_ref, f32[2,40,128]{2,1,0:T(8,128)S(1)} %get-tuple-element.150.tab_ref, ...), custom_call_target="tpu_custom_call" | custom-call | tf_op jit(solution)/shard_map/cond/branch_0_fun/update_1/pallas_call | solution.py:475
  164.5 0.0 copy-start
  164.5 2.8 %copy.29 = bf16[1,1,2048,384]{3,2,1,0:T(8,128)(2,1)} copy(bf16[1,1,2048,384]{3,2,1,0:T(8,128)(2,1)} %bitcast.29) | data formatting | bytes 3145728
  167.3 0.8 copy.30
  168.1 0.0 copy-done
  168.1 0.0 copy-start.1
  168.1 1.1 copy.31
  169.3 0.3 copy-done.1
  169.5 0.8 copy.32
  (5 shorter events, 0.0 us)
Async XLA Ops:
  164.5 3.6 %copy-start = (bf16[2048,384]{1,0:T(8,128)(2,1)S(1)}, bf16[2048,384]{1,0:T(8,128)(2,1)}, u32[]{:S(2)}) copy-start(bf16[2048,384]{1,0:T(8,128)(2,1)} %get-tuple-element.193) | copy-start | bytes 4718596
  168.1 1.4 copy-start.1
